TPU v7x, 1024 devices: a whole 8x8x8 slice. The times are simulated.
1024 devices in a mesh: tile: 16 (over z_lo, y), date: 64 (over z_hi, x, core).
Axes of the slice: x: 8, y: 8, z: 8 (z_hi: 4, z_lo: 2; z = z_hi * 2 + z_lo), core: 2. Of those that a mesh axis runs over, the one named last changes fastest.
Arguments:
- layer_input: bfloat16 [1024, 256, 1024], P('tile', 'date'), may hold values from -6 to 6
- head_input: bfloat16 [1024, 256, 1024], P('tile', 'date'), may hold values from -6 to 6
- out_grad: bfloat16 [1024, 256, 1024], P('tile', 'date'), may hold values from -6 to 6
- sensor_ids: int32 [256], P('date'), may hold values from 0 to 1
- valid_mask: int32 [1024, 256], P('tile', 'date'), may hold values 0 or 1
- sensor_table: float32 [2, 1024], replicated, may hold values from -4 to 4
- proj_weight: bfloat16 [1024, 264], replicated, may hold values from -0.09375 to 0.09375
- step_bias: float32 [8], replicated, may hold values from -4 to -2
- decay_log: float32 [8], replicated, may hold values from -4 to 0
- skip_gain: float32 [8], replicated, may hold values from 0.5 to 1.5
Outputs:
- value_grad: bfloat16 [1024, 256, 1024], P('tile', 'date')
- input_grad: bfloat16 [1024, 256, 1024], P('tile', 'date')
- weight_grad: float32 [1024, 264], replicated
- table_grad: float32 [2, 1024], replicated
- head_grads: float32 [3, 8], replicated
All inputs are finite; a program needn't handle non-finite values. No bound on the sum of `valid_mask` on one device may be relied on, other than what follows from the above.
Results may differ from a plain program's by a relative error of at most 0.0088.
Values may be sent and summed in bfloat16 or wider, within the bound.
A program may use at most 64 MiB of HBM per device.

v0:
```python
import math

import jax
import jax.numpy as jnp
from jax import lax
from jax.sharding import PartitionSpec as P

SPAN = 64


HIGHEST_PREC = lax.Precision.HIGHEST
NEG_FILL = -1e30


def span_scan(values_in, keys_in, reads_in, step_in, decay_in, skip_in, block_len):
    series, length, head_count, width_p = values_in.shape
    states_n = keys_in.shape[2]
    block_count = length // block_len
    decay_rate = -jnp.exp(decay_in)
    values_blk = values_in.reshape(series, block_count, block_len, head_count, width_p)
    keys_b = keys_in.reshape(series, block_count, block_len, states_n)
    reads_c = reads_in.reshape(series, block_count, block_len, states_n)
    step_blocks = step_in.reshape(series, block_count, block_len, head_count)
    weighted = values_blk * step_blocks[..., None]
    log_decay = jnp.cumsum(step_blocks * decay_rate, axis=2)
    log_heads = jnp.swapaxes(log_decay, 2, 3)
    row_ids = lax.broadcasted_iota(jnp.int32, (block_len, block_len), 0)
    col_ids = lax.broadcasted_iota(jnp.int32, (block_len, block_len), 1)
    causal = row_ids >= col_ids
    gap_logs = log_heads[..., :, None] - log_heads[..., None, :]
    kernel = jnp.exp(jnp.where(causal, gap_logs, NEG_FILL))
    scores = jnp.einsum("scin,scjn->scij", reads_c, keys_b, precision=HIGHEST_PREC)
    mixed_kernel = kernel * scores[:, :, None]
    within_block = jnp.einsum("schij,scjhp->scihp", mixed_kernel, weighted, precision=HIGHEST_PREC)
    to_block_end = jnp.exp(log_decay[:, :, -1:, :] - log_decay)
    block_states = jnp.einsum(
        "scjn,scjhp->schnp", keys_b, weighted * to_block_end[..., None], precision=HIGHEST_PREC
    )
    block_totals = jnp.exp(log_decay[:, :, -1, :])

    def advance(state_carry, block_item):
        block_total, block_state = block_item
        return (state_carry * block_total[:, :, None, None] + block_state, state_carry)

    zero_state = jnp.zeros((series, head_count, states_n, width_p), dtype=values_in.dtype)
    _, entering = lax.scan(
        advance, zero_state, (jnp.moveaxis(block_totals, 1, 0), jnp.moveaxis(block_states, 1, 0))
    )
    entering = jnp.moveaxis(entering, 0, 1)
    from_earlier = (
        jnp.einsum("scin,schnp->scihp", reads_c, entering, precision=HIGHEST_PREC)
        * jnp.exp(log_decay)[..., None]
    )
    result = within_block + from_earlier + skip_in[:, None] * values_blk
    return result.reshape(series, length, head_count, width_p)


def on_device(
    layer_input,
    head_input,
    out_grad,
    sensor_ids,
    valid_mask,
    sensor_table,
    proj_weight,
    step_bias,
    decay_log,
    skip_gain,
):
    pixel_dev, dates_dev, model_d = layer_input.shape
    head_count = step_bias.shape[0]
    width_hp = head_input.shape[2]
    width_p = width_hp // head_count
    states_n = (proj_weight.shape[1] - head_count) // 2
    is_second = (sensor_ids == 1)[None, :, None]
    sensor_embed = jnp.where(is_second, sensor_table[1], sensor_table[0])
    mixed_in = (layer_input.astype(jnp.float32) + sensor_embed).astype(jnp.bfloat16)
    flat_in = mixed_in.reshape(pixel_dev * dates_dev, model_d)
    projected = jnp.dot(flat_in, proj_weight, preferred_element_type=jnp.float32).reshape(
        pixel_dev, dates_dev, -1
    )
    pair_proj = projected[:, :, : 2 * states_n].astype(jnp.bfloat16)
    step_pre = projected[:, :, 2 * states_n :] + step_bias
    valid_gate = valid_mask.astype(jnp.float32)[:, :, None]
    step_sizes = (valid_gate * jax.nn.softplus(step_pre)).astype(jnp.bfloat16)

    def local_scan(values_in, keys_in, reads_in, step_in, decay_in, skip_in):
        return span_scan(
            values_in, keys_in, reads_in, step_in, decay_in, skip_in, min(SPAN, values_in.shape[1])
        )

    series_values, series_cot, series_pairs, series_steps = (
        lax.all_to_all(head_input, "date", split_axis=0, concat_axis=1, tiled=True),
        lax.all_to_all(out_grad, "date", split_axis=0, concat_axis=1, tiled=True),
        lax.all_to_all(pair_proj, "date", split_axis=0, concat_axis=1, tiled=True),
        lax.all_to_all(step_sizes, "date", split_axis=0, concat_axis=1, tiled=True),
    )
    series_count = series_values.shape[0]
    length = series_values.shape[1]
    _, pullback = jax.vjp(
        local_scan,
        series_values.astype(jnp.float32).reshape(series_count, length, head_count, width_p),
        series_pairs[..., :states_n].astype(jnp.float32),
        series_pairs[..., states_n:].astype(jnp.float32),
        series_steps.astype(jnp.float32),
        decay_log,
        skip_gain,
    )
    series_count = series_values.shape[0]
    length = series_values.shape[1]
    grad_values, grad_b, grad_c, grad_steps, grad_decay, grad_skip = pullback(
        series_cot.astype(jnp.float32).reshape(series_count, length, head_count, width_p)
    )
    value_series = grad_values.reshape(series_count, length, width_hp).astype(jnp.bfloat16)
    pair_series = jnp.concatenate([grad_b, grad_c], axis=-1).astype(jnp.bfloat16)
    step_series = grad_steps.astype(jnp.bfloat16)
    value_grad, pair_grad, step_grad = (
        lax.all_to_all(value_series, "date", split_axis=1, concat_axis=0, tiled=True),
        lax.all_to_all(pair_series, "date", split_axis=1, concat_axis=0, tiled=True),
        lax.all_to_all(step_series, "date", split_axis=1, concat_axis=0, tiled=True),
    )
    raw_grad = step_grad.astype(jnp.float32) * valid_gate * jax.nn.sigmoid(step_pre)
    proj_grad = jnp.concatenate([pair_grad, raw_grad.astype(jnp.bfloat16)], axis=-1).reshape(
        pixel_dev * dates_dev, -1
    )
    weight_part = lax.dot_general(
        flat_in, proj_grad, (((0,), (0,)), ((), ())), preferred_element_type=jnp.float32
    )
    flat_grad = lax.dot_general(
        proj_grad, proj_weight, (((1,), (1,)), ((), ())), preferred_element_type=jnp.float32
    )
    input_grad = flat_grad.astype(jnp.bfloat16).reshape(pixel_dev, dates_dev, model_d)
    flat_back = flat_grad.reshape(pixel_dev, dates_dev, model_d)
    second_sum = jnp.sum(jnp.where(is_second, flat_back, 0.0), axis=(0, 1))
    first_sum = jnp.sum(jnp.where(is_second, 0.0, flat_back), axis=(0, 1))
    table_part = jnp.stack([first_sum, second_sum])
    head_part = jnp.stack([grad_decay, jnp.sum(raw_grad, axis=(0, 1)), grad_skip])
    weight_sum, table_sum, head_sum = lax.psum(
        (weight_part, table_part, head_part), ("tile", "date")
    )
    total_tokens = pixel_dev * dates_dev * lax.axis_size("tile") * lax.axis_size("date")
    grad_scale = 1.0 / math.sqrt(total_tokens)
    return (
        value_grad,
        input_grad,
        weight_sum * grad_scale,
        table_sum * grad_scale,
        head_sum * grad_scale,
    )


def solution(mesh):
    in_specs = (
        P("tile", "date", None),
        P("tile", "date", None),
        P("tile", "date", None),
        P("date"),
        P("tile", "date"),
        P(),
        P(),
        P(),
        P(),
        P(),
    )
    out_specs = (P("tile", "date", None), P("tile", "date", None), P(), P(), P())
    return jax.shard_map(
        on_device, mesh=mesh, in_specs=in_specs, out_specs=out_specs, check_vma=False
    )
```

profile of v0, /device:TPU:1, one launch (start us, length us, event | category | flops | bytes accessed | tf_op | source)
XLA Modules:
  0.0 542.2 jit_solution(2773537823171886263)
XLA Ops:
  12.2 22.7 %all-to-all-start.1 = ((bf16[64,4,8]{2,1,0:T(4,128)(2,1)}), bf16[64,4,8]{2,1,0:T(4,128)(2,1)S(1)}, u32[]{:S(2)}, u32[]{:S(2)}) async-start(bf16[64,4,8]{2,1,0:T(4,128)(2,1)} %copy.235), calls=%async_computation.1 | async-start | bytes 131072 | tf_op jit(solution)/shard_map/all_to_all | solution.py:96
  35.8 11.4 %all-to-all-done.1 = bf16[64,4,8]{2,1,0:T(4,128)(2,1)S(1)} async-done(((bf16[64,4,8]{2,1,0:T(4,128)(2,1)}), bf16[64,4,8]{2,1,0:T(4,128)(2,1)S(1)}, u32[]{:S(2)}, u32[]{:S(2)}) %all-to-all-start.1) | async-done | bytes 4128 | tf_op jit(solution)/shard_map/all_to_all | solution.py:96
  47.2 4.4 all-to-all-start.2
  51.7 12.8 %all-to-all-done.2 = bf16[64,4,256]{2,1,0:T(4,128)(2,1)S(1)} async-done(((bf16[64,4,256]{2,1,0:T(4,128)(2,1)}), bf16[64,4,256]{2,1,0:T(4,128)(2,1)S(1)}, u32[]{:S(2)}, u32[]{:S(2)}) %all-to-all-start.2) | async-done | bytes 131104 | tf_op jit(solution)/shard_map/all_to_all | solution.py:95
  64.5 4.5 all-to-all-start.3
  73.4 14.4 %all-to-all-done.3 = bf16[64,4,1024]{2,1,0:T(4,128)(2,1)S(1)} async-done(((bf16[64,4,1024]{2,1,0:T(4,128)(2,1)}), bf16[64,4,1024]{2,1,0:T(4,128)(2,1)S(1)}, u32[]{:S(2)}, u32[]{:S(2)}) %all-to-all-start.3) | async-done | bytes 524320 | tf_op jit(solution)/shard_map/all_to_all | solution.py:93
  87.8 8.5 %all-to-all-start = ((bf16[64,4,1024]{2,1,0:T(4,128)(2,1)}), bf16[64,4,1024]{2,1,0:T(4,128)(2,1)}, u32[]{:S(2)}, u32[]{:S(2)}) async-start(bf16[64,4,1024]{2,1,0:T(4,128)(2,1)} %param.16), calls=%async_computation | async-start | bytes 1048576 | tf_op jit(solution)/shard_map/all_to_all | solution.py:94
  96.5 3.7 convolution_bitcast_fusion
  101.7 20.8 %while.34 = (s32[]{:T(128)}, f32[1,8,128,128]{3,2,1,0:T(8,128)S(1)}, f32[4,1,8,128,128]{4,3,2,1,0:T(8,128)}, f32[4,1,8,1,1]{2,4,3,1,0:T(1,128)}, f32[4,1,8]{2,1,...) while((s32[]{:T(128)}, f32[1,8,128,128]{3,2,1,0:T(8,128)S(1)}, ...), condition=%wide.region_2.3_spmd.clone, body=%wide.region_1.2_spmd.clone.sunk | while | flops 524291 | bytes 4720840 | solution.py:46
  124.1 3.2 convolution_bitcast_fusion.1
  128.9 2.3 fusion.24
  132.9 16.7 %while.35 = (s32[]{:T(128)}, f32[1,8,128,128]{3,2,1,0:T(8,128)S(1)}, f32[4,1,8]{2,1,0:T(1,128)S(1)}, f32[4,1,8,128,128]{4,3,2,1,0:T(8,128)}, f32[4,1,8,128,128]{...) while((s32[]{:T(128)}, ...), condition=%wide.region_5.6_spmd.clone, body=%wide.region_3.5_spmd.clone.sunk | while | flops 786428 | bytes 5244176 | solution.py:46
  150.2 2.5 fusion.11
  154.7 3.2 fusion.40
  159.1 4.7 multiply_reduce_fusion.2
  170.8 13.1 %all-to-all-start.6 = ((bf16[1,256,8]{2,0,1:T(2,128)(2,1)}), bf16[1,256,8]{2,0,1:T(2,128)(2,1)S(1)}, u32[]{:S(2)}, u32[]{:S(2)}) async-start(bf16[1,256,8]{2,0,1:T(2,128)(2,1)} %copy.269), calls=%async_computation.6 | async-start | bytes 262144 | tf_op jit(solution)/shard_map/all_to_all | solution.py:120
  185.0 4.1 fusion.30
  194.9 3.7 reduce.35
  199.7 12.7 %all-to-all-start.5 = ((bf16[64,2,512]{2,1,0:T(2,128)(2,1)}), bf16[64,2,512]{2,1,0:T(2,128)(2,1)S(1)}, u32[]{:S(2)}, u32[]{:S(2)}) async-start(bf16[64,2,512]{2,1,0:T(2,128)(2,1)} %reshape.609), calls=%async_computation.5 | async-start | bytes 262144 | tf_op jit(solution)/shard_map/all_to_all | solution.py:119
  213.2 12.0 %all-to-all-done.5 = bf16[64,2,512]{2,1,0:T(2,128)(2,1)S(1)} async-done(((bf16[64,2,512]{2,1,0:T(2,128)(2,1)}), bf16[64,2,512]{2,1,0:T(2,128)(2,1)S(1)}, u32[]{:S(2)}, u32[]{:S(2)}) %all-to-all-start.5) | async-done | bytes 131104 | tf_op jit(solution)/shard_map/all_to_all | solution.py:119
  225.2 4.5 all-to-all-start.4
  233.8 118.7 %all-reduce.2 = (f32[2,1024]{1,0:T(2,128)S(1)}, f32[3,8]{1,0:T(4,128)S(1)}) all-reduce(f32[2,1024]{1,0:T(2,128)S(1)} %pad_maximum_fusion.1, f32[3,8]{1,0:T(4,128)S(1)} %pad_maximum_fusion.2), channel_id=1, replica_groups=mesh['tile'=16,'date'=64] {'tile','date'}, use_global_device_ids=true, to_apply=%region_17.18 | all-reduce | flops 2072 | bytes 16576 | tf_op jit(solution)/shard_map/psum | solution.py:138
  353.6 174.6 %all-reduce.5.cloned.1.call-done = f32[1024,264]{0,1:T(8,128)} async-done(((f32[1024,264]{0,1:T(8,128)}), f32[1024,264]{0,1:T(8,128)}) %all-reduce.5.cloned.1.call-update) | async-done | bytes 1081360 | tf_op jit(solution)/shard_map/psum | solution.py:138
  531.2 3.0 bitcast_reduce_fusion.1
  (178 shorter events, 81.7 us)
Async XLA Ops:
  7.2 3.6 copy-start
  7.2 4.2 copy-start.16
  7.2 4.2 copy-start.13
  7.2 44.4 %copy-start.18 = (f32[8]{0:T(128)S(1)}, f32[8]{0:T(128)}, u32[]{:S(2)}) copy-start(f32[8]{0:T(128)} %param.22) | copy-start | bytes 100
  10.0 0.8 copy-start.4
  11.4 0.9 copy-start.10
  12.2 34.9 %all-to-all-start.1 = ((bf16[64,4,8]{2,1,0:T(4,128)(2,1)}), bf16[64,4,8]{2,1,0:T(4,128)(2,1)S(1)}, u32[]{:S(2)}, u32[]{:S(2)}) async-start(bf16[64,4,8]{2,1,0:T(4,128)(2,1)} %copy.235), calls=%async_computation.1 | async-start | bytes 131072 | tf_op jit(solution)/shard_map/all_to_all | solution.py:96
  47.2 17.3 %all-to-all-start.2 = ((bf16[64,4,256]{2,1,0:T(4,128)(2,1)}), bf16[64,4,256]{2,1,0:T(4,128)(2,1)S(1)}, u32[]{:S(2)}, u32[]{:S(2)}) async-start(bf16[64,4,256]{2,1,0:T(4,128)(2,1)} %copy.238), calls=%async_computation.2 | async-start | bytes 262144 | tf_op jit(solution)/shard_map/all_to_all | solution.py:95
  51.6 18.6 %copy-start.15 = (f32[8]{0:T(128)}, f32[8]{0:T(128)S(1)}, u32[]{:S(2)}) copy-start(f32[8]{0:T(128)S(1)} %exponential_negate_fusion) | copy-start | bytes 100
  64.5 23.3 %all-to-all-start.3 = ((bf16[64,4,1024]{2,1,0:T(4,128)(2,1)}), bf16[64,4,1024]{2,1,0:T(4,128)(2,1)S(1)}, u32[]{:S(2)}, u32[]{:S(2)}) async-start(bf16[64,4,1024]{2,1,0:T(4,128)(2,1)} %param.15), calls=%async_computation.3 | async-start | bytes 1048576 | tf_op jit(solution)/shard_map/all_to_all | solution.py:93
  87.8 34.7 %all-to-all-start = ((bf16[64,4,1024]{2,1,0:T(4,128)(2,1)}), bf16[64,4,1024]{2,1,0:T(4,128)(2,1)}, u32[]{:S(2)}, u32[]{:S(2)}) async-start(bf16[64,4,1024]{2,1,0:T(4,128)(2,1)} %param.16), calls=%async_computation | async-start | bytes 1048576 | tf_op jit(solution)/shard_map/all_to_all | solution.py:94
  96.5 5.2 copy-start.2
  124.1 3.2 copy-start.1
  150.2 4.6 copy-start.3
  170.8 18.5 %copy-start.6 = (f32[4,64,64]{1,2,0:T(8,128)S(1)}, f32[4,64,64]{1,2,0:T(8,128)}, u32[]{:S(2)}) copy-start(f32[4,64,64]{1,2,0:T(8,128)} %get-tuple-element.322) | copy-start | bytes 196612
  170.8 29.0 %all-to-all-start.6 = ((bf16[1,256,8]{2,0,1:T(2,128)(2,1)}), bf16[1,256,8]{2,0,1:T(2,128)(2,1)S(1)}, u32[]{:S(2)}, u32[]{:S(2)}) async-start(bf16[1,256,8]{2,0,1:T(2,128)(2,1)} %copy.269), calls=%async_computation.6 | async-start | bytes 262144 | tf_op jit(solution)/shard_map/all_to_all | solution.py:120
  189.2 5.1 copy-start.7
  194.6 18.1 %copy-start.11 = (f32[64,4]{0,1:T(4,128)S(1)}, f32[64,4]{0,1:T(4,128)}, u32[]{:S(2)}) copy-start(f32[64,4]{0,1:T(4,128)} %copy-done.10) | copy-start | bytes 3076
  194.6 18.1 %copy-start.14 = (f32[8]{0:T(128)S(1)}, f32[8]{0:T(128)}, u32[]{:S(2)}) copy-start(f32[8]{0:T(128)} %param.21) | copy-start | bytes 100
  198.6 32.3 %copy-start.5 = (bf16[64,4,1024]{2,1,0:T(4,128)(2,1)S(1)}, bf16[64,4,1024]{2,1,0:T(4,128)(2,1)}, u32[]{:S(2)}) copy-start(bf16[64,4,1024]{2,1,0:T(4,128)(2,1)} %copy-done.4) | copy-start | bytes 1572868
  199.7 25.5 %all-to-all-start.5 = ((bf16[64,2,512]{2,1,0:T(2,128)(2,1)}), bf16[64,2,512]{2,1,0:T(2,128)(2,1)S(1)}, u32[]{:S(2)}, u32[]{:S(2)}) async-start(bf16[64,2,512]{2,1,0:T(2,128)(2,1)} %reshape.609), calls=%async_computation.5 | async-start | bytes 262144 | tf_op jit(solution)/shard_map/all_to_all | solution.py:119
  225.2 305.4 %all-to-all-start.4 = ((bf16[64,2,2048]{2,1,0:T(2,128)(2,1)}), bf16[64,2,2048]{2,1,0:T(2,128)(2,1)S(1)}, u32[]{:S(2)}, u32[]{:S(2)}) async-start(bf16[64,2,2048]{2,1,0:T(2,128)(2,1)} %reshape.607), calls=%async_computation.4 | async-start | bytes 1048576 | tf_op jit(solution)/shard_map/all_to_all | solution.py:118
  229.7 298.6 %all-reduce.5.cloned.1.call-start = ((), (), s32[]{:S(2)}) async-start(), calls=%async_computation.7 | async-start | bytes 2162688 | tf_op jit(solution)/shard_map/psum | solution.py:138
  230.1 2.2 copy-start.17
  (3 other events, 1.8 us)
Sparse Core Ops, SparseCore 0:
  235.9 292.3 all-reduce.4
where the time goes:
time: 548 us; the launch traced here: 542 us
  waiting for transfers between devices  225 us (41%)
  blocking collectives  119 us (22%)
  starting transfers between devices  70.8 us (13%)
  local copies, waits for them, and re-layouts  49.7 us (9%)
  other arithmetic  32.3 us (6%)
  matrix products  30 us (5%)
  between operations  14.8 us (3%)
    psum x1, waiting for transfers between devices, on_device(): lax.psum((weight_part, table_part, head_part), ('tile', 'date'))  175 us
    psum x1, blocking collectives, on_device(): lax.psum((weight_part, table_part, head_part), ('tile', 'date'))  119 us
    all_to_all x1, starting transfers between devices, on_device(): lax.all_to_all(step_sizes, 'date', split_axis=0, concat_axis=1, tiled=True)  22.7 us
    all_to_all x1, waiting for transfers between devices, on_device(): lax.all_to_all(head_input, 'date', split_axis=0, concat_axis=1, tiled=True)  14.4 us
    all_to_all x1, starting transfers between devices, on_device(): lax.all_to_all(step_series, 'date', split_axis=1, concat_axis=0, tiled=True)  13.1 us
    all_to_all x1, waiting for transfers between devices, on_device(): lax.all_to_all(pair_proj, 'date', split_axis=0, concat_axis=1, tiled=True)  12.8 us
    all_to_all x1, starting transfers between devices, on_device(): lax.all_to_all(pair_series, 'date', split_axis=1, concat_axis=0, tiled=True)  12.7 us
    all_to_all x1, waiting for transfers between devices, on_device(): lax.all_to_all(pair_series, 'date', split_axis=1, concat_axis=0, tiled=True)  12 us
  transfers between devices with their start and end apart: 8, of which 5 were waited for; matrix products, arithmetic and copies ran while one was open for 10% of the time, Pallas kernels for 0%

commit v1 on v0

v1 whole, which is shorter than its diff:
```python
import math

import jax
import jax.numpy as jnp
from jax import lax
from jax.experimental import pallas as pl
from jax.experimental.pallas import tpu as pltpu
from jax.sharding import PartitionSpec as P

F32 = jnp.float32
BF16 = jnp.bfloat16
NEG_FILL = -1e30
NT = 64
RING = 8
LEN = 256


def mm(a, b, dims):
    return lax.dot_general(a, b, (dims, ((), ())), preferred_element_type=F32)


def iota(shape, dim):
    return lax.broadcasted_iota(jnp.int32, shape, dim)


def body(
    scale,
    li, xh, yh, ids, valid, table, wt, bias, decay, skip,
    vg, ig, wg, tg, hg,
    libuf, mix, wdt, gate, psend,
    pair, xb, yb, l_s, lt_s, dtt_s, g_s, dg_s, r_s, p_s, sk_s, dd_s, vs, pgs,
    pgr, igs, wfull, s0, r0, s1, r1, a1, s2, r2, s3, r3, q2, q1, p0,
    a0s, a0r, a1s, a1r, a2s, a2r, a3s, a3r, d4s, d4r,
    lsem, own_sem, ss, rs, fs, fr,
):
    tile = lax.axis_index("tile")
    me = lax.axis_index("date")
    core = lax.rem(me, 2)
    cx = lax.rem(me // 2, RING)
    zh = me // (2 * RING)
    cy = lax.rem(tile, RING)
    zl = tile // RING
    cz = zh * 2 + zl
    fi = (1 - core) * cx + core * cy
    se = core * cx + (1 - core) * cy

    def at(x, y, z, c):
        return (lax.rem(z, 2) * RING + y, ((z // 2) * RING + x) * 2 + c)

    def first_peer(f):
        return at((1 - core) * f + core * cx, core * f + (1 - core) * cy, cz, core)

    def second_peer(s):
        return at(core * s + (1 - core) * cx, (1 - core) * s + core * cy, cz, core)

    def x_peer(x):
        return at(x, cy, cz, core)

    def y_peer(y):
        return at(cx, y, cz, core)

    def z_peer(z):
        return at(cx, cy, z, core)

    partner = at(cx, cy, cz, 1 - core)

    def ring(n, mine, step):
        def one(k, carry):
            step(lax.rem(mine + k, n))
            return carry

        lax.fori_loop(1, n, one, 0)

    def send(src, dst, i, to, recv=None):
        pltpu.make_async_remote_copy(
            src_ref=src, dst_ref=dst, send_sem=ss.at[i], recv_sem=rs.at[i] if recv is None else recv,
            device_id=to, device_id_type=pl.DeviceIdType.MESH,
        ).start()

    def drain(ref, sem):
        pltpu.make_async_copy(ref, ref, sem).wait()

    barrier = pltpu.get_barrier_semaphore()

    def greet(to):
        pl.semaphore_signal(barrier, inc=1, device_id=to, device_id_type=pl.DeviceIdType.MESH)

    ring(NT, me, lambda d: greet((tile, d)))
    ring(RING, cy, lambda y: greet(y_peer(y)))

    def greet_z(k, carry):
        greet(at(cx, cy, 2 * k + 1 - zl, core))
        return carry

    lax.fori_loop(0, RING // 2, greet_z, 0)

    loads = [pltpu.make_async_copy(li.at[:, k], libuf.at[k], lsem.at[k]) for k in range(8)]
    for c in loads:
        c.start()
    own_x = pltpu.make_async_copy(xh.at[me], xb.at[:, me], own_sem.at[0])
    own_y = pltpu.make_async_copy(yh.at[me], yb.at[:, me], own_sem.at[1])
    own_x.start()
    own_y.start()
    row = iota((LEN, 128), 0)
    lane = iota((LEN, 128), 1)
    r3i = row & 3
    sens = jnp.where(r3i == 0, ids[0], jnp.where(r3i == 1, ids[1], jnp.where(r3i == 2, ids[2], ids[3])))
    is2 = sens == 1
    lif = libuf.reshape(8, LEN, 128)
    for k in range(8):
        loads[k].wait()
        cols = slice(128 * k, 128 * (k + 1))
        emb = jnp.where(is2, table[1:2, cols], table[0:1, cols])
        mix[:, cols] = (lif[k].astype(F32) + emb).astype(BF16)
    wdt[...] = jnp.zeros_like(wdt)
    wdt[0:8, :] = wt[256:264, :]
    pairs = mm(mix[...], wt[0:256, :], ((1,), (1,)))
    pre = mm(mix[...], wdt[...], ((1,), (1,)))
    lane1 = iota((1, 128), 1)
    bias_row = jnp.zeros((1, 128), F32)
    dec_row = jnp.zeros((1, 128), F32)
    for h in range(8):
        bias_row = jnp.where(lane1 == h, bias[h], bias_row)
        dec_row = jnp.where(lane1 == h, decay[h], dec_row)
    pre = pre + bias_row
    row6 = iota((LEN, NT), 0)
    col6 = iota((LEN, NT), 1)
    val = jnp.zeros((LEN, NT), F32)
    for t in range(4):
        val = jnp.where(((row6 >> 2) == col6) & ((row6 & 3) == t), valid[t : t + 1, :].astype(F32), val)
    val = jnp.sum(val, axis=1, keepdims=True)
    steps = jnp.where(lane < 8, val * jax.nn.softplus(pre), 0.0)
    gate[...] = jnp.where(lane < 8, val * jax.nn.sigmoid(pre), 0.0)
    psf = psend.reshape(3, LEN, 128)
    psf[0] = pairs[:, 0:128].astype(BF16)
    psf[1] = pairs[:, 128:256].astype(BF16)
    psf[2] = steps.astype(BF16)
    own_p = pltpu.make_async_copy(psend.at[:, me], pair.at[:, me], own_sem.at[2])
    own_p.start()

    pl.semaphore_wait(barrier, (NT - 1) + (RING - 1) + RING // 2)

    def forward(d):
        send(psend.at[:, d], pair.at[:, me], 0, (tile, d))
        send(yh.at[d], yb.at[:, me], 1, (tile, d))
        send(xh.at[d], xb.at[:, me], 2, (tile, d))

    ring(NT, me, forward)

    i2 = iota((LEN, LEN), 0)
    j2 = iota((LEN, LEN), 1)
    a_row = -jnp.exp(dec_row)
    row8 = iota((8, 128), 0)
    lane8 = iota((8, 128), 1)
    a_col = jnp.sum(jnp.where(row8 == lane8, a_row, 0.0), axis=1, keepdims=True)
    tril = (i2 >= j2).astype(F32).astype(BF16)
    strict = (i2 < j2).astype(F32).astype(BF16)
    eye = (i2 == j2).astype(F32).astype(BF16)
    dg_s[...] = jnp.zeros_like(dg_s)
    dd_s[...] = jnp.zeros_like(dd_s)

    own_p.wait()
    drain(pair.at[:, pl.ds(0, NT - 1)], rs.at[0])
    pf = pair.reshape(3, LEN, 128)
    dtb = pf[2]
    l_s[...] = mm(tril, dtb, ((1,), (0,))) * a_row
    lt_s[...] = mm(dtb, tril, ((0,), (1,)))[0:8, :] * a_col
    dtt_s[...] = mm(dtb, eye, ((0,), (0,)))[0:8, :]
    g_s[...] = mm(pf[1], pf[0], ((1,), (1,)))

    own_x.wait()
    own_y.wait()
    drain(yb.at[:, pl.ds(0, NT - 1)], rs.at[1])
    drain(xb.at[:, pl.ds(0, NT - 1)], rs.at[2])
    xf = xb.reshape(8, LEN, 128)
    yf = yb.reshape(8, LEN, 128)
    vf = vs.reshape(8, LEN, 128)

    def head(h, carry):
        pick = lane == h
        lc = jnp.sum(jnp.where(pick, l_s[...], 0.0), axis=1, keepdims=True)
        dtc = jnp.sum(jnp.where(pick, pf[2].astype(F32), 0.0), axis=1, keepdims=True)
        lr = lt_s[pl.ds(h, 1), :]
        dtr = dtt_s[pl.ds(h, 1), :]
        ker = jnp.exp(jnp.where(i2 >= j2, lc - lr, NEG_FILL))
        x = xf[h]
        y = yf[h]
        kz = ker * mm(y, x, ((1,), (1,)))
        dg_s[...] += kz * dtr
        g = g_s[...]
        both = kz * g
        p_s[pl.ds(h, 1), :] = jnp.sum(both, axis=0, keepdims=True)
        spread = mm((both * dtr).astype(BF16), strict, ((1,), (0,)))
        r_s[pl.ds(h, 1), :] = jnp.sum(jnp.where(i2 >= j2, spread, 0.0), axis=0, keepdims=True)
        dw = mm((ker * g).astype(BF16), y, ((0,), (0,)))
        y32 = y.astype(F32)
        vf[h] = (dw * dtc + skip[h] * y32).astype(BF16)
        sk_s[pl.ds(h, 1), :] = jnp.sum(y32 * x.astype(F32), axis=0, keepdims=True)
        return carry

    lax.fori_loop(0, 8, head, 0)
    pgf = pgs.reshape(3, LEN, 128)
    dgb = dg_s[...].astype(BF16)
    pgf[0] = mm(dgb, pf[1], ((0,), (0,))).astype(BF16)
    pgf[1] = mm(dgb, pf[0], ((1,), (0,))).astype(BF16)
    dd_s[0:8, :] = a_col * r_s[...] + p_s[...]
    pgf[2] = jnp.transpose(dd_s[...]).astype(BF16)
    own_g = pltpu.make_async_copy(pgs.at[:, me], pgr.at[:, me], own_sem.at[3])
    own_g.start()
    ring(NT, me, lambda d: send(pgs.at[:, d], pgr.at[:, me], 3, (tile, d)))
    own_v = pltpu.make_async_copy(vs.at[:, me], vg.at[me], own_sem.at[4])
    own_v.start()
    ring(NT, me, lambda d: send(vs.at[:, d], vg.at[me], 4, (tile, d)))
    decay_col = a_col * jnp.sum(r_s[...] * dtt_s[...], axis=1, keepdims=True)
    skip_col = jnp.sum(sk_s[...], axis=1, keepdims=True)
    head_row = jnp.sum(
        jnp.where(lane8 == row8, decay_col, 0.0) + jnp.where(lane8 == row8 + 64, skip_col, 0.0), axis=0, keepdims=True
    )

    own_g.wait()
    drain(pgr.at[:, pl.ds(0, NT - 1)], rs.at[3])
    prf = pgr.reshape(3, LEN, 128)
    raw = prf[2].astype(F32) * gate[...]
    rawb = raw.astype(BF16)
    gb = prf[0]
    gc = prf[1]
    wb = mm(gb, mix[...], ((0,), (0,)))
    wc = mm(gc, mix[...], ((0,), (0,)))
    for k in range(8):
        cols = slice(128 * k, 128 * (k + 1))
        wfull[0, k] = wb[:, cols]
        wfull[1, k] = wc[:, cols]
    s0[...] = wfull[1 - core].astype(BF16)
    send(s0, r0, 5, partner)
    wd = mm(rawb, mix[...], ((0,), (0,)))
    for k in range(8):
        a0s[k] = wd[0:8, 128 * k : 128 * (k + 1)]
    tok = iota((8, LEN), 1) & 3
    sens8 = jnp.where(tok == 0, ids[0], jnp.where(tok == 1, ids[1], jnp.where(tok == 2, ids[2], ids[3])))
    rows8 = iota((8, LEN), 0)
    sel = jnp.where(rows8 < 3, (sens8 != 1).astype(F32), jnp.where(rows8 < 6, (sens8 == 1).astype(F32), 0.0)).astype(BF16)
    sum_b = mm(sel, gb, ((1,), (0,)))
    sum_c = mm(sel, gc, ((1,), (0,)))
    sum_r = mm(sel, rawb, ((1,), (0,)))
    raw_sum = jnp.sum(raw, axis=0, keepdims=True)
    kind = jnp.where(row8 < 3, row8, row8 - 3)
    small = jnp.where(kind == 0, sum_b, jnp.where(kind == 1, sum_c, sum_r))
    small = jnp.where(row8 == 6, head_row, jnp.where(row8 == 7, raw_sum, small))
    a0s[8] = small
    send(a0s, a0r, 6, partner)

    drain(r0, rs.at[5])
    for k in range(8):
        both = wfull[core, k] + r0[k].astype(F32)
        wfull[core, k] = both
        s1[k] = both.astype(BF16)
    ring(RING, fi, lambda f: send(s1.at[f], r1.at[fi], 7, first_peer(f)))
    drain(a0r, rs.at[6])
    for k in range(8):
        a1s[k, 0] = a0s[k] + a0r[k]
        a1s[k, 1] = a0s[8] + a0r[8]
    a1r[cx] = a1s[cx]
    ring(RING, cx, lambda x: send(a1s.at[x], a1r.at[cx], 8, x_peer(x)))

    flat = mm(gb, wt[0:128, :], ((1,), (0,))) + mm(gc, wt[128:256, :], ((1,), (0,))) + mm(rawb, wdt[...], ((1,), (0,)))
    igf = igs.reshape(8, LEN, 128)
    for k in range(8):
        igf[k] = flat[:, 128 * k : 128 * (k + 1)].astype(BF16)
    stores = [pltpu.make_async_copy(igs.at[k], ig.at[:, k], lsem.at[k]) for k in range(8)]
    for c in stores:
        c.start()

    drain(r1.at[pl.ds(0, RING - 1)], rs.at[7])
    a1[...] = wfull[core, fi]

    def add1(k, carry):
        a1[...] += r1[lax.rem(fi + k, RING)].astype(F32)
        return carry

    lax.fori_loop(1, RING, add1, 0)
    s2[...] = a1[...].astype(BF16).reshape(RING, 16, 128)
    ring(RING, se, lambda s: send(s2.at[s], r2.at[se], 9, second_peer(s)))
    drain(a1r.at[pl.ds(0, RING - 1)], rs.at[8])
    a2s[...] = ((a1r[0] + a1r[1]) + (a1r[2] + a1r[3])) + ((a1r[4] + a1r[5]) + (a1r[6] + a1r[7]))
    a2r[cy] = a2s[...]
    ring(RING, cy, lambda y: send(a2s, a2r.at[cy], 10, y_peer(y)))

    drain(r2.at[pl.ds(0, RING - 1)], rs.at[9])
    s3[...] = a1[pl.ds(pl.multiple_of(se * 16, 16), 16), :]

    def add2(k, carry):
        s3[...] += r2[lax.rem(se + k, RING)].astype(F32)
        return carry

    lax.fori_loop(1, RING, add2, 0)
    r3[cz] = s3[...]
    ring(RING, cz, lambda z: send(s3, r3.at[cz], 11, z_peer(z)))
    drain(a2r.at[pl.ds(0, RING - 1)], rs.at[10])
    a3s[...] = ((a2r[0] + a2r[1]) + (a2r[2] + a2r[3])) + ((a2r[4] + a2r[5]) + (a2r[6] + a2r[7]))
    a3r[cz] = a3s[...]
    ring(RING, cz, lambda z: send(a3s, a3r.at[cz], 12, z_peer(z)))

    drain(r3.at[pl.ds(0, RING - 1)], rs.at[11])
    total = ((r3[0] + r3[1]) + (r3[2] + r3[3])) + ((r3[4] + r3[5]) + (r3[6] + r3[7]))
    q2[se] = (total * scale).astype(BF16)
    ring(RING, se, lambda s: send(q2.at[se], q2.at[se], 13, second_peer(s)))
    drain(a3r.at[pl.ds(0, RING - 1)], rs.at[12])
    aux = ((a3r[0] + a3r[1]) + (a3r[2] + a3r[3])) + ((a3r[4] + a3r[5]) + (a3r[6] + a3r[7]))
    aux = aux * scale
    d4s[...] = aux[0]
    d4r[cx] = aux[0]
    ring(RING, cx, lambda x: send(d4s, d4r.at[cx], 14, x_peer(x)))
    small = aux[1]

    drain(q2.at[pl.ds(0, RING - 1)], rs.at[13])
    send(q2, p0.at[fi], 15, partner, fr.at[fi])
    ring(RING, fi, lambda f: send(q2, q1.at[fi], 16, first_peer(f), fs.at[fi]))
    q1[fi] = q2[...]

    hi = small.astype(BF16)
    left = small - hi.astype(F32)
    mid = left.astype(BF16)
    low = (left - mid.astype(F32)).astype(BF16)

    def times(w):
        return mm(hi, w, ((1,), (0,))) + (mm(mid, w, ((1,), (0,))) + mm(low, w, ((1,), (0,))))

    tb = times(wt[0:128, :])
    tc = times(wt[128:256, :])
    tr = times(wdt[...])
    tg[0:1, :] = tb[0:1] + tc[1:2] + tr[2:3]
    tg[1:2, :] = tb[3:4] + tc[4:5] + tr[5:6]
    hg[0:1, :] = small[6:7, 0:8]
    hg[1:2, :] = small[7:8, 0:8]
    hg[2:3, :] = pltpu.roll(small, 64, 1)[6:7, 0:8]
    drain(d4r.at[pl.ds(0, RING - 1)], rs.at[14])
    for k in range(8):
        wg[256:264, 128 * k : 128 * (k + 1)] = d4r[k]

    def pass_on(f):
        drain(q1.at[f], fs.at[f])
        send(q1.at[f], p0.at[f], 15, partner, fr.at[f])

    ring(RING, fi, pass_on)
    mine = pl.multiple_of(core * 128, 128)
    other = pl.multiple_of((1 - core) * 128, 128)
    for k in range(8):
        wg[pl.ds(mine, 128), 128 * k : 128 * (k + 1)] = q1[k].reshape(128, 128).astype(F32)
    for k in range(8):
        drain(p0.at[k], fr.at[k])
        wg[pl.ds(other, 128), 128 * k : 128 * (k + 1)] = p0[k].reshape(128, 128).astype(F32)

    own_v.wait()
    drain(vs.at[:, pl.ds(0, NT - 1)], rs.at[4])
    for c in stores:
        c.wait()
    drain(psend.at[:, pl.ds(0, NT - 1)], ss.at[0])
    drain(yb.at[:, pl.ds(0, NT - 1)], ss.at[1])
    drain(xb.at[:, pl.ds(0, NT - 1)], ss.at[2])
    drain(pgs.at[:, pl.ds(0, NT - 1)], ss.at[3])
    drain(vs.at[:, pl.ds(0, NT - 1)], ss.at[4])
    drain(s0, ss.at[5])
    drain(a0s, ss.at[6])
    drain(s1.at[pl.ds(0, RING - 1)], ss.at[7])
    drain(a1s.at[pl.ds(0, RING - 1)], ss.at[8])
    drain(s2.at[pl.ds(0, RING - 1)], ss.at[9])
    drain(a2r.at[pl.ds(0, RING - 1)], ss.at[10])
    drain(r3.at[pl.ds(0, RING - 1)], ss.at[11])
    drain(a3r.at[pl.ds(0, RING - 1)], ss.at[12])
    drain(q2.at[pl.ds(0, RING - 1)], ss.at[13])
    drain(d4r.at[pl.ds(0, RING - 1)], ss.at[14])
    drain(p0, ss.at[15])
    drain(q1.at[pl.ds(0, RING - 1)], ss.at[16])


def on_device(layer_input, head_input, out_grad, sensor_ids, valid_mask, sensor_table, proj_weight, step_bias, decay_log, skip_gain):
    pixels, dates, width = layer_input.shape
    total = pixels * dates * lax.axis_size("tile") * lax.axis_size("date")

    def heads(a):
        return a.reshape(pixels, dates, 8, 128).transpose(0, 2, 1, 3)

    any_ = pl.BlockSpec(memory_space=pl.ANY)
    vm = pl.BlockSpec(memory_space=pltpu.VMEM)
    sm = pl.BlockSpec(memory_space=pltpu.SMEM)
    four = (8, NT, 4, 128)

    def v(shape, dtype):
        return pltpu.VMEM(shape, dtype)

    scratch = [
        v(four, BF16), v((LEN, 1024), BF16), v((128, 1024), BF16), v((LEN, 128), F32), v((3, NT, 4, 128), BF16),
        v((3, NT, 4, 128), BF16), v(four, BF16), v(four, BF16), v((LEN, 128), F32), v((8, LEN), F32), v((8, LEN), F32),
        v((LEN, LEN), F32), v((LEN, LEN), F32), v((8, LEN), F32), v((8, LEN), F32), v((8, 128), F32), v((128, LEN), F32),
        v(four, BF16), v((3, NT, 4, 128), BF16),
        v((3, NT, 4, 128), BF16), v(four, BF16), v((2, 8, 128, 128), F32), v((8, 128, 128), BF16), v((8, 128, 128), BF16),
        v((8, 128, 128), BF16), v((8, 128, 128), BF16), v((128, 128), F32), v((8, 16, 128), BF16), v((8, 16, 128), BF16),
        v((16, 128), F32), v((8, 16, 128), F32), v((8, 16, 128), BF16), v((8, 8, 16, 128), BF16), v((8, 8, 16, 128), BF16),
        v((9, 8, 128), F32), v((9, 8, 128), F32), v((8, 2, 8, 128), F32), v((8, 2, 8, 128), F32), v((2, 8, 128), F32),
        v((8, 2, 8, 128), F32), v((2, 8, 128), F32), v((8, 2, 8, 128), F32), v((8, 128), F32), v((8, 8, 128), F32),
        pltpu.SemaphoreType.DMA((8,)), pltpu.SemaphoreType.DMA((5,)), pltpu.SemaphoreType.DMA((17,)),
        pltpu.SemaphoreType.DMA((15,)), pltpu.SemaphoreType.DMA((8,)), pltpu.SemaphoreType.DMA((8,)),
    ]

    def kernel(*refs):
        body(1.0 / math.sqrt(total), *refs)

    vg, ig, wg, tg, hg = pl.pallas_call(
        kernel,
        name="mixer_backward",
        out_shape=(
            jax.ShapeDtypeStruct((pixels, 8, dates, 128), BF16),
            jax.ShapeDtypeStruct((pixels, 8, dates, 128), BF16),
            jax.ShapeDtypeStruct((264, 1024), F32),
            jax.ShapeDtypeStruct((2, 1024), F32),
            jax.ShapeDtypeStruct((3, 8), F32),
        ),
        in_specs=[any_, any_, any_, sm, vm, vm, vm, sm, sm, sm],
        out_specs=(any_, any_, vm, vm, vm),
        scratch_shapes=scratch,
        compiler_params=pltpu.CompilerParams(collective_id=0, has_side_effects=True),
    )(
        heads(layer_input), heads(head_input), heads(out_grad), sensor_ids, valid_mask.T, sensor_table, proj_weight.T,
        step_bias, decay_log, skip_gain,
    )

    def dates_first(a):
        return a.transpose(0, 2, 1, 3).reshape(pixels, dates, width)

    return dates_first(vg), dates_first(ig), wg.T, tg, hg


def solution(mesh):
    in_specs = (
        P("tile", "date", None), P("tile", "date", None), P("tile", "date", None), P("date"), P("tile", "date"),
        P(), P(), P(), P(), P(),
    )
    out_specs = (P("tile", "date", None), P("tile", "date", None), P(), P(), P())
    return jax.shard_map(on_device, mesh=mesh, in_specs=in_specs, out_specs=out_specs, check_vma=False)
```

time: 548 us -> 131 us (0.24); the launches traced: 542 us -> 131 us
  waiting for transfers between devices: 225 us -> 0 us
  Pallas kernels: 0 us -> 124 us
  blocking collectives: 119 us -> 0 us
  starting transfers between devices: 70.8 us -> 0 us
  local copies, waits for them, and re-layouts: 49.7 us -> 6.29 us
  other arithmetic: 32.3 us -> 0 us
  matrix products: 30 us -> 0 us
  between operations: 14.8 us -> 0.66 us
    psum x1 -> x0, waiting for transfers between devices: 175 us -> none  [on_device(): lax.psum((weight_part, table_part, head_part), ('tile', 'date'))]
    pallas_call x0 -> x1, Pallas kernels: none -> 124 us  [on_device(): pl.pallas_call(kernel, name='mixer_backward', out_shape=(jax.ShapeDtypeSt...]
    psum x1 -> x0, blocking collectives: 119 us -> none  [on_device(): lax.psum((weight_part, table_part, head_part), ('tile', 'date'))]
    all_to_all x7 -> x0, starting transfers between devices: 70.5 us -> none  [the longest x1 22.7 us: on_device(): lax.all_to_all(step_sizes, 'date', split_axis=0, concat_axis=1, tiled=True)]
    all_to_all x7 -> x0, waiting for transfers between devices: 50.7 us -> none  [the longest x1 14.4 us: on_device(): lax.all_to_all(head_input, 'date', split_axis=0, concat_axis=1, tiled=True)]
    dot_general x14 -> x0, matrix products: 30 us -> none  [the longest x3 10.3 us: span_scan(): jnp.einsum('scjn,scjhp->schnp', keys_b, weighted * to_block_end[..., None...]
    dynamic_slice x16 -> x0, local copies, waits for them, and re-layouts: 10.2 us -> none  [span_scan(): lax.scan(advance, zero_state, (jnp.moveaxis(block_totals, 1, 0), jnp.move...]
    mul x8 -> x0, local copies, waits for them, and re-layouts: 7.34 us -> none  [advance(): state_carry * block_total[:, :, None, None] + block_state]
  transfers between devices with their start and end apart: 8 -> 0, of which waited for: 5 -> 0; matrix products, arithmetic and copies ran while one was open for 10% -> 0% of each run, Pallas kernels for 0% -> 0%
where the time goes in v1:
time: 131 us
  Pallas kernels  124 us (95%)
  local copies, waits for them, and re-layouts  6.29 us (5%)
    pallas_call x1, Pallas kernels, on_device(): pl.pallas_call(kernel, name='mixer_backward', out_shape=(jax.ShapeDtypeSt...  124 us
    unnamed x11, local copies, waits for them, and re-layouts  6.29 us

profile of v1, /device:TPU:1, one launch (start us, length us, event | category | flops | bytes accessed | tf_op | source)
XLA Modules:
  0.0 130.8 jit_solution(11337856008431838646)
XLA Ops:
  0.6 123.9 %mixer_backward.1 = (bf16[64,8,4,128]{3,2,1,0:T(4,128)(2,1)}, bf16[64,8,4,128]{3,2,1,0:T(4,128)(2,1)}, f32[264,1024]{1,0:T(8,128)}, f32[2,1024]{1,0:T(2,128)}, f32[3,8]{1,0:T(4,128)}) custom-call(bf16[64,8,4,128]{3,2,1,0:T(4,128)(2,1)} %bitcast.22, bf16[64,8,4,128]{3,2,1,0:T(4,128)(2,1)} %bitcast.23, bf16[64,8,4,128]{3,2,1,0:T(4,128)(2,1)} %bitcast.24, ...), custom_call_target="tpu_custom_call" | custom-call | tf_op jit(solution)/shard_map/mixer_backward/pallas_call | solution.py:408
  124.5 0.0 copy-start
  124.5 2.1 %copy.20 = bf16[64,4,1024]{2,1,0:T(4,128)(2,1)} copy(bf16[64,4,1024]{2,1,0:T(4,128)(2,1)} %bitcast.21) | data formatting | bytes 1048576
  126.6 2.0 %copy.21 = bf16[64,4,1024]{2,1,0:T(4,128)(2,1)} copy(bf16[64,4,1024]{2,1,0:T(4,128)(2,1)} %bitcast.20) | data formatting | bytes 1048576
  128.6 0.0 copy-done
  128.6 0.0 copy-start.1
  128.6 0.0 copy-start.2
  128.6 1.0 copy.22
  129.6 0.0 copy-done.1
  129.6 0.6 copy.23
  130.2 0.0 copy-done.2
  130.2 0.6 copy.24
Async XLA Ops:
  124.5 4.1 %copy-start = (f32[264,1024]{1,0:T(8,128)S(1)}, f32[264,1024]{1,0:T(8,128)}, u32[]{:S(2)}) copy-start(f32[264,1024]{1,0:T(8,128)} %get-tuple-element.12) | copy-start | bytes 3244036
  128.6 1.0 copy-start.1
  128.6 1.6 %copy-start.2 = (f32[3,8]{1,0:T(4,128)S(1)}, f32[3,8]{1,0:T(4,128)}, u32[]{:S(2)}) copy-start(f32[3,8]{1,0:T(4,128)} %get-tuple-element.24) | copy-start | bytes 292

commit v2 on v1

--- a/solution.py
+++ b/solution.py
@@ -12,6 +12,8 @@
 NEG_FILL = -1e30
 NT = 64
 RING = 8
+EARLY = 6
+OWN = 46
 LEN = 256
 
 
@@ -25,13 +27,14 @@
 
 def body(
     scale,
-    li, xh, yh, ids, valid, table, wt, bias, decay, skip,
+    li, xh, yh, ids_h, valid_h, table_h, wt_h, bias_h, decay_h, skip_h,
     vg, ig, wg, tg, hg,
+    ids, valid, table, wt, bias, decay, skip,
     libuf, mix, wdt, gate, psend,
     pair, xb, yb, l_s, lt_s, dtt_s, g_s, dg_s, r_s, p_s, sk_s, dd_s, vs, pgs,
-    pgr, igs, wfull, s0, r0, s1, r1, a1, s2, r2, s3, r3, q2, q1, p0,
+    pgr, wfull, s0, r0, s1, r1, a1, s2, r2, s3, r3, q2, q1, p0,
     a0s, a0r, a1s, a1r, a2s, a2r, a3s, a3r, d4s, d4r,
-    lsem, own_sem, ss, rs, fs, fr,
+    in_sem, lsem, own_sem, ss, rs, fs, fr,
 ):
     tile = lax.axis_index("tile")
     me = lax.axis_index("date")
@@ -71,6 +74,22 @@
 
         lax.fori_loop(1, n, one, 0)
 
+    def offset(n):
+        return ((n + 1) // 2) * (1 - 2 * lax.rem(n, 2))
+
+    def far_first(low, high, step):
+        def one(k, carry):
+            v = lax.rem(k // 2, 4)
+            u = lax.rem(k // 8 + 2 * RING - 2 * v, RING)
+            z = lax.rem(zh + 2 + offset(v) + 4, 4)
+            x = lax.rem(cx + RING // 2 + offset(u) + RING, RING)
+            step((z * RING + x) * 2 + lax.rem(core + k, 2))
+            return carry
+
+        for a, b in ((low, min(high, OWN)), (max(low, OWN + 1), high)):
+            if a < b:
+                lax.fori_loop(a, b, one, 0)
+
     def send(src, dst, i, to, recv=None):
         pltpu.make_async_remote_copy(
             src_ref=src, dst_ref=dst, send_sem=ss.at[i], recv_sem=rs.at[i] if recv is None else recv,
@@ -85,7 +104,7 @@
     def greet(to):
         pl.semaphore_signal(barrier, inc=1, device_id=to, device_id_type=pl.DeviceIdType.MESH)
 
-    ring(NT, me, lambda d: greet((tile, d)))
+    far_first(0, NT, lambda d: greet((tile, d)))
     ring(RING, cy, lambda y: greet(y_peer(y)))
 
     def greet_z(k, carry):
@@ -94,6 +113,14 @@
 
     lax.fori_loop(0, RING // 2, greet_z, 0)
 
+    smalls = [
+        pltpu.make_async_copy(a, b, in_sem.at[i])
+        for i, (a, b) in enumerate((
+            (ids_h, ids), (valid_h, valid), (table_h, table), (wt_h, wt), (bias_h, bias), (decay_h, decay), (skip_h, skip),
+        ))
+    ]
+    for c in smalls:
+        c.start()
     loads = [pltpu.make_async_copy(li.at[:, k], libuf.at[k], lsem.at[k]) for k in range(8)]
     for c in loads:
         c.start()
@@ -101,6 +128,11 @@
     own_y = pltpu.make_async_copy(yh.at[me], yb.at[:, me], own_sem.at[1])
     own_x.start()
     own_y.start()
+    pl.semaphore_wait(barrier, (NT - 1) + (RING - 1) + RING // 2)
+    far_first(0, NT, lambda d: send(yh.at[d], yb.at[:, me], 1, (tile, d)))
+
+    for c in smalls:
+        c.wait()
     row = iota((LEN, 128), 0)
     lane = iota((LEN, 128), 1)
     r3i = row & 3
@@ -138,14 +170,9 @@
     own_p = pltpu.make_async_copy(psend.at[:, me], pair.at[:, me], own_sem.at[2])
     own_p.start()
 
-    pl.semaphore_wait(barrier, (NT - 1) + (RING - 1) + RING // 2)
-
-    def forward(d):
-        send(psend.at[:, d], pair.at[:, me], 0, (tile, d))
-        send(yh.at[d], yb.at[:, me], 1, (tile, d))
-        send(xh.at[d], xb.at[:, me], 2, (tile, d))
-
-    ring(NT, me, forward)
+    far_first(0, NT, lambda d: send(psend.at[:, d], pair.at[:, me], 0, (tile, d)))
+    far_first(0, NT, lambda d: send(xh.at[d, pl.ds(0, EARLY)], xb.at[pl.ds(0, EARLY), me], 2, (tile, d)))
+    far_first(0, NT, lambda d: send(xh.at[d, pl.ds(EARLY, 8 - EARLY)], xb.at[pl.ds(EARLY, 8 - EARLY), me], 17, (tile, d)))
 
     i2 = iota((LEN, LEN), 0)
     j2 = iota((LEN, LEN), 1)
@@ -171,7 +198,7 @@
     own_x.wait()
     own_y.wait()
     drain(yb.at[:, pl.ds(0, NT - 1)], rs.at[1])
-    drain(xb.at[:, pl.ds(0, NT - 1)], rs.at[2])
+    drain(xb.at[pl.ds(0, EARLY), pl.ds(0, NT - 1)], rs.at[2])
     xf = xb.reshape(8, LEN, 128)
     yf = yb.reshape(8, LEN, 128)
     vf = vs.reshape(8, LEN, 128)
@@ -198,7 +225,9 @@
         sk_s[pl.ds(h, 1), :] = jnp.sum(y32 * x.astype(F32), axis=0, keepdims=True)
         return carry
 
-    lax.fori_loop(0, 8, head, 0)
+    lax.fori_loop(0, EARLY, head, 0)
+    drain(xb.at[pl.ds(EARLY, 8 - EARLY), pl.ds(0, NT - 1)], rs.at[17])
+    lax.fori_loop(EARLY, 8, head, 0)
     pgf = pgs.reshape(3, LEN, 128)
     dgb = dg_s[...].astype(BF16)
     pgf[0] = mm(dgb, pf[1], ((0,), (0,))).astype(BF16)
@@ -207,10 +236,14 @@
     pgf[2] = jnp.transpose(dd_s[...]).astype(BF16)
     own_g = pltpu.make_async_copy(pgs.at[:, me], pgr.at[:, me], own_sem.at[3])
     own_g.start()
-    ring(NT, me, lambda d: send(pgs.at[:, d], pgr.at[:, me], 3, (tile, d)))
+    far_first(0, NT, lambda d: send(pgs.at[:, d], pgr.at[:, me], 3, (tile, d)))
     own_v = pltpu.make_async_copy(vs.at[:, me], vg.at[me], own_sem.at[4])
     own_v.start()
-    ring(NT, me, lambda d: send(vs.at[:, d], vg.at[me], 4, (tile, d)))
+
+    def give_values(low, high):
+        far_first(low, high, lambda d: send(vs.at[:, d], vg.at[me], 4, (tile, d)))
+
+    give_values(0, 28)
     decay_col = a_col * jnp.sum(r_s[...] * dtt_s[...], axis=1, keepdims=True)
     skip_col = jnp.sum(sk_s[...], axis=1, keepdims=True)
     head_row = jnp.sum(
@@ -224,14 +257,13 @@
     rawb = raw.astype(BF16)
     gb = prf[0]
     gc = prf[1]
-    wb = mm(gb, mix[...], ((0,), (0,)))
-    wc = mm(gc, mix[...], ((0,), (0,)))
-    for k in range(8):
-        cols = slice(128 * k, 128 * (k + 1))
-        wfull[0, k] = wb[:, cols]
-        wfull[1, k] = wc[:, cols]
-    s0[...] = wfull[1 - core].astype(BF16)
+    give = mm(prf[1 - core], mix[...], ((0,), (0,)))
+    for k in range(8):
+        s0[k] = give[:, 128 * k : 128 * (k + 1)].astype(BF16)
     send(s0, r0, 5, partner)
+    keep = mm(prf[core], mix[...], ((0,), (0,)))
+    for k in range(8):
+        wfull[k] = keep[:, 128 * k : 128 * (k + 1)]
     wd = mm(rawb, mix[...], ((0,), (0,)))
     for k in range(8):
         a0s[k] = wd[0:8, 128 * k : 128 * (k + 1)]
@@ -251,8 +283,8 @@
 
     drain(r0, rs.at[5])
     for k in range(8):
-        both = wfull[core, k] + r0[k].astype(F32)
-        wfull[core, k] = both
+        both = wfull[k] + r0[k].astype(F32)
+        wfull[k] = both
         s1[k] = both.astype(BF16)
     ring(RING, fi, lambda f: send(s1.at[f], r1.at[fi], 7, first_peer(f)))
     drain(a0r, rs.at[6])
@@ -262,16 +294,18 @@
     a1r[cx] = a1s[cx]
     ring(RING, cx, lambda x: send(a1s.at[x], a1r.at[cx], 8, x_peer(x)))
 
-    flat = mm(gb, wt[0:128, :], ((1,), (0,))) + mm(gc, wt[128:256, :], ((1,), (0,))) + mm(rawb, wdt[...], ((1,), (0,)))
-    igf = igs.reshape(8, LEN, 128)
-    for k in range(8):
-        igf[k] = flat[:, 128 * k : 128 * (k + 1)].astype(BF16)
-    stores = [pltpu.make_async_copy(igs.at[k], ig.at[:, k], lsem.at[k]) for k in range(8)]
-    for c in stores:
-        c.start()
+    igf = ig.reshape(8, LEN, 128)
+
+    def input_grad(low, high):
+        for k in range(low, high):
+            cols = slice(128 * k, 128 * (k + 1))
+            flat = mm(gb, wt[0:128, cols], ((1,), (0,))) + mm(gc, wt[128:256, cols], ((1,), (0,)))
+            igf[k] = (flat + mm(rawb, wdt[:, cols], ((1,), (0,)))).astype(BF16)
+
+    input_grad(0, 2)
 
     drain(r1.at[pl.ds(0, RING - 1)], rs.at[7])
-    a1[...] = wfull[core, fi]
+    a1[...] = wfull[fi]
 
     def add1(k, carry):
         a1[...] += r1[lax.rem(fi + k, RING)].astype(F32)
@@ -284,6 +318,8 @@
     a2s[...] = ((a1r[0] + a1r[1]) + (a1r[2] + a1r[3])) + ((a1r[4] + a1r[5]) + (a1r[6] + a1r[7]))
     a2r[cy] = a2s[...]
     ring(RING, cy, lambda y: send(a2s, a2r.at[cy], 10, y_peer(y)))
+    give_values(28, 40)
+    input_grad(2, 4)
 
     drain(r2.at[pl.ds(0, RING - 1)], rs.at[9])
     s3[...] = a1[pl.ds(pl.multiple_of(se * 16, 16), 16), :]
@@ -299,6 +335,8 @@
     a3s[...] = ((a2r[0] + a2r[1]) + (a2r[2] + a2r[3])) + ((a2r[4] + a2r[5]) + (a2r[6] + a2r[7]))
     a3r[cz] = a3s[...]
     ring(RING, cz, lambda z: send(a3s, a3r.at[cz], 12, z_peer(z)))
+    give_values(40, 52)
+    input_grad(4, 6)
 
     drain(r3.at[pl.ds(0, RING - 1)], rs.at[11])
     total = ((r3[0] + r3[1]) + (r3[2] + r3[3])) + ((r3[4] + r3[5]) + (r3[6] + r3[7]))
@@ -310,6 +348,8 @@
     d4s[...] = aux[0]
     d4r[cx] = aux[0]
     ring(RING, cx, lambda x: send(d4s, d4r.at[cx], 14, x_peer(x)))
+    give_values(52, NT)
+    input_grad(6, 8)
     small = aux[1]
 
     drain(q2.at[pl.ds(0, RING - 1)], rs.at[13])
@@ -352,11 +392,10 @@
 
     own_v.wait()
     drain(vs.at[:, pl.ds(0, NT - 1)], rs.at[4])
-    for c in stores:
-        c.wait()
     drain(psend.at[:, pl.ds(0, NT - 1)], ss.at[0])
     drain(yb.at[:, pl.ds(0, NT - 1)], ss.at[1])
-    drain(xb.at[:, pl.ds(0, NT - 1)], ss.at[2])
+    drain(xb.at[pl.ds(0, EARLY), pl.ds(0, NT - 1)], ss.at[2])
+    drain(xb.at[pl.ds(EARLY, 8 - EARLY), pl.ds(0, NT - 1)], ss.at[17])
     drain(pgs.at[:, pl.ds(0, NT - 1)], ss.at[3])
     drain(vs.at[:, pl.ds(0, NT - 1)], ss.at[4])
     drain(s0, ss.at[5])
@@ -373,6 +412,18 @@
     drain(q1.at[pl.ds(0, RING - 1)], ss.at[16])
 
 
+def write_out(vi, ii, wi, ti, hi, vo, io, wo, to, ho, sem):
+    pieces = [(vi.at[pl.ds(16 * n, 16)], vo.at[pl.ds(16 * n, 16)]) for n in range(4)]
+    pieces += [(ii.at[k], io.at[:, k]) for k in range(8)]
+    pieces += [(wi.at[pl.ds(88 * n, 88)], wo.at[pl.ds(88 * n, 88)]) for n in range(3)]
+    pieces += [(ti, to), (hi, ho)]
+    puts = [pltpu.make_async_copy(a, b, sem.at[i]) for i, (a, b) in enumerate(pieces)]
+    for c in puts:
+        c.start()
+    for c in puts:
+        c.wait()
+
+
 def on_device(layer_input, head_input, out_grad, sensor_ids, valid_mask, sensor_table, proj_weight, step_bias, decay_log, skip_gain):
     pixels, dates, width = layer_input.shape
     total = pixels * dates * lax.axis_size("tile") * lax.axis_size("date")
@@ -382,24 +433,25 @@
 
     any_ = pl.BlockSpec(memory_space=pl.ANY)
     vm = pl.BlockSpec(memory_space=pltpu.VMEM)
-    sm = pl.BlockSpec(memory_space=pltpu.SMEM)
     four = (8, NT, 4, 128)
 
     def v(shape, dtype):
         return pltpu.VMEM(shape, dtype)
 
+    sm = pltpu.SMEM
     scratch = [
+        sm((4,), jnp.int32), v((4, NT), jnp.int32), v((2, 1024), F32), v((264, 1024), BF16), sm((8,), F32), sm((8,), F32), sm((8,), F32),
         v(four, BF16), v((LEN, 1024), BF16), v((128, 1024), BF16), v((LEN, 128), F32), v((3, NT, 4, 128), BF16),
         v((3, NT, 4, 128), BF16), v(four, BF16), v(four, BF16), v((LEN, 128), F32), v((8, LEN), F32), v((8, LEN), F32),
         v((LEN, LEN), F32), v((LEN, LEN), F32), v((8, LEN), F32), v((8, LEN), F32), v((8, 128), F32), v((128, LEN), F32),
         v(four, BF16), v((3, NT, 4, 128), BF16),
-        v((3, NT, 4, 128), BF16), v(four, BF16), v((2, 8, 128, 128), F32), v((8, 128, 128), BF16), v((8, 128, 128), BF16),
+        v((3, NT, 4, 128), BF16), v((8, 128, 128), F32), v((8, 128, 128), BF16), v((8, 128, 128), BF16),
         v((8, 128, 128), BF16), v((8, 128, 128), BF16), v((128, 128), F32), v((8, 16, 128), BF16), v((8, 16, 128), BF16),
         v((16, 128), F32), v((8, 16, 128), F32), v((8, 16, 128), BF16), v((8, 8, 16, 128), BF16), v((8, 8, 16, 128), BF16),
         v((9, 8, 128), F32), v((9, 8, 128), F32), v((8, 2, 8, 128), F32), v((8, 2, 8, 128), F32), v((2, 8, 128), F32),
         v((8, 2, 8, 128), F32), v((2, 8, 128), F32), v((8, 2, 8, 128), F32), v((8, 128), F32), v((8, 8, 128), F32),
-        pltpu.SemaphoreType.DMA((8,)), pltpu.SemaphoreType.DMA((5,)), pltpu.SemaphoreType.DMA((17,)),
-        pltpu.SemaphoreType.DMA((15,)), pltpu.SemaphoreType.DMA((8,)), pltpu.SemaphoreType.DMA((8,)),
+        pltpu.SemaphoreType.DMA((7,)), pltpu.SemaphoreType.DMA((8,)), pltpu.SemaphoreType.DMA((5,)), pltpu.SemaphoreType.DMA((18,)),
+        pltpu.SemaphoreType.DMA((18,)), pltpu.SemaphoreType.DMA((8,)), pltpu.SemaphoreType.DMA((8,)),
     ]
 
     def kernel(*refs):
@@ -409,20 +461,27 @@
         kernel,
         name="mixer_backward",
         out_shape=(
-            jax.ShapeDtypeStruct((pixels, 8, dates, 128), BF16),
-            jax.ShapeDtypeStruct((pixels, 8, dates, 128), BF16),
-            jax.ShapeDtypeStruct((264, 1024), F32),
-            jax.ShapeDtypeStruct((2, 1024), F32),
-            jax.ShapeDtypeStruct((3, 8), F32),
+            v((pixels, 8, dates, 128), BF16), v(four, BF16), v((264, 1024), F32),
+            v((2, 1024), F32), v((3, 8), F32),
         ),
-        in_specs=[any_, any_, any_, sm, vm, vm, vm, sm, sm, sm],
-        out_specs=(any_, any_, vm, vm, vm),
+        in_specs=[any_] * 10,
+        out_specs=(vm, vm, vm, vm, vm),
         scratch_shapes=scratch,
         compiler_params=pltpu.CompilerParams(collective_id=0, has_side_effects=True),
     )(
         heads(layer_input), heads(head_input), heads(out_grad), sensor_ids, valid_mask.T, sensor_table, proj_weight.T,
         step_bias, decay_log, skip_gain,
     )
+
+    six = jax.ShapeDtypeStruct((pixels, 8, dates, 128), BF16)
+    vg, ig, wg, tg, hg = pl.pallas_call(
+        write_out,
+        name="write_outputs",
+        out_shape=(six, six, *(jax.ShapeDtypeStruct(a.shape, a.dtype) for a in (wg, tg, hg))),
+        in_specs=[vm] * 5,
+        out_specs=(any_,) * 5,
+        scratch_shapes=[pltpu.SemaphoreType.DMA((17,))],
+    )(*(pltpu.with_memory_space_constraint(a, pltpu.VMEM) for a in (vg, ig, wg, tg, hg)))
 
     def dates_first(a):
         return a.transpose(0, 2, 1, 3).reshape(pixels, dates, width)

time: 131 us -> 107 us (0.82)
  Pallas kernels: 124 us -> 106 us
  local copies, waits for them, and re-layouts: 6.29 us -> 0 us
    pallas_call x1 -> x2, Pallas kernels: 124 us -> 106 us  [the longest x1 105 us: on_device(): pl.pallas_call(kernel, name='mixer_backward', out_shape=(v((pixels, 8, da...]
    unnamed x11 -> x0, local copies, waits for them, and re-layouts: 6.29 us -> none
where the time goes in v2:
time: 107 us
  Pallas kernels  106 us (99%)
    pallas_call x1, Pallas kernels, on_device(): pl.pallas_call(kernel, name='mixer_backward', out_shape=(v((pixels, 8, da...  105 us

profile of v2, /device:TPU:1, one launch (start us, length us, event | category | flops | bytes accessed | tf_op | source)
XLA Modules:
  0.0 106.7 jit_solution(595444706061030427)
XLA Ops:
  0.6 104.6 %mixer_backward.1 = (bf16[64,8,4,128]{3,2,1,0:T(4,128)(2,1)S(1)}, bf16[8,64,4,128]{3,2,1,0:T(4,128)(2,1)S(1)}, f32[264,1024]{1,0:T(8,128)S(1)}, f32[2,1024]{1,0:T(2,128)S(1)}, f32[3,8]{1,0:T(4,128)S(1)}) custom-call(bf16[64,8,4,128]{3,2,1,0:T(4,128)(2,1)} %bitcast.19, bf16[64,8,4,128]{3,2,1,0:T(4,128)(2,1)} %bitcast.20, bf16[64,8,4,128]{3,2,1,0:T(4,128)(2,1)} %bitcast.21, ...), custom_call_target="tpu_custom_call" | custom-call | tf_op jit(solution)/shard_map/mixer_backward/pallas_call | solution.py:460
  105.3 1.5 %write_outputs.1 = (bf16[64,8,4,128]{3,2,1,0:T(4,128)(2,1)}, bf16[64,8,4,128]{3,2,1,0:T(4,128)(2,1)}, f32[264,1024]{1,0:T(8,128)}, f32[2,1024]{1,0:T(2,128)}, f32[3,8]{1,0:T(4,128)}) custom-call(bf16[64,8,4,128]{3,2,1,0:T(4,128)(2,1)S(1)} %get-tuple-element.15.vi, bf16[8,64,4,128]{3,2,1,0:T(4,128)(2,1)S(1)} %get-tuple-element.16.ii, ...), custom_call_target="tpu_custom_call" | custom-call | tf_op jit(solution)/shard_map/write_outputs/pallas_call | solution.py:477

commit v3 on v2

--- a/solution.py
+++ b/solution.py
@@ -67,22 +67,32 @@
 
     partner = at(cx, cy, cz, 1 - core)
 
-    def ring(n, mine, step):
-        def one(k, carry):
-            step(lax.rem(mine + k, n))
-            return carry
-
-        lax.fori_loop(1, n, one, 0)
-
     def offset(n):
         return ((n + 1) // 2) * (1 - 2 * lax.rem(n, 2))
+
+    def chip(mine, u):
+        return lax.rem(mine + RING // 2 + offset(u) + RING, RING)
+
+    def ring(mine, step):
+        def one(u, carry):
+            step(chip(mine, u))
+            return carry
+
+        lax.fori_loop(0, RING - 1, one, 0)
+
+    def near_ring(mine, step):
+        def one(u, carry):
+            step(chip(mine, RING - 2 - u))
+            return carry
+
+        lax.fori_loop(0, RING - 1, one, 0)
 
     def far_first(low, high, step):
         def one(k, carry):
             v = lax.rem(k // 2, 4)
             u = lax.rem(k // 8 + 2 * RING - 2 * v, RING)
             z = lax.rem(zh + 2 + offset(v) + 4, 4)
-            x = lax.rem(cx + RING // 2 + offset(u) + RING, RING)
+            x = chip(cx, u)
             step((z * RING + x) * 2 + lax.rem(core + k, 2))
             return carry
 
@@ -105,7 +115,7 @@
         pl.semaphore_signal(barrier, inc=1, device_id=to, device_id_type=pl.DeviceIdType.MESH)
 
     far_first(0, NT, lambda d: greet((tile, d)))
-    ring(RING, cy, lambda y: greet(y_peer(y)))
+    ring(cy, lambda y: greet(y_peer(y)))
 
     def greet_z(k, carry):
         greet(at(cx, cy, 2 * k + 1 - zl, core))
@@ -286,13 +296,13 @@
         both = wfull[k] + r0[k].astype(F32)
         wfull[k] = both
         s1[k] = both.astype(BF16)
-    ring(RING, fi, lambda f: send(s1.at[f], r1.at[fi], 7, first_peer(f)))
+    ring(fi, lambda f: send(s1.at[f], r1.at[fi], 7, first_peer(f)))
     drain(a0r, rs.at[6])
     for k in range(8):
         a1s[k, 0] = a0s[k] + a0r[k]
         a1s[k, 1] = a0s[8] + a0r[8]
-    a1r[cx] = a1s[cx]
-    ring(RING, cx, lambda x: send(a1s.at[x], a1r.at[cx], 8, x_peer(x)))
+    a1r[cz] = a1s[cz]
+    ring(cz, lambda z: send(a1s.at[z], a1r.at[cz], 8, z_peer(z)))
 
     igf = ig.reshape(8, LEN, 128)
 
@@ -313,11 +323,11 @@
 
     lax.fori_loop(1, RING, add1, 0)
     s2[...] = a1[...].astype(BF16).reshape(RING, 16, 128)
-    ring(RING, se, lambda s: send(s2.at[s], r2.at[se], 9, second_peer(s)))
+    ring(se, lambda s: send(s2.at[s], r2.at[se], 9, second_peer(s)))
     drain(a1r.at[pl.ds(0, RING - 1)], rs.at[8])
     a2s[...] = ((a1r[0] + a1r[1]) + (a1r[2] + a1r[3])) + ((a1r[4] + a1r[5]) + (a1r[6] + a1r[7]))
     a2r[cy] = a2s[...]
-    ring(RING, cy, lambda y: send(a2s, a2r.at[cy], 10, y_peer(y)))
+    ring(cy, lambda y: send(a2s, a2r.at[cy], 10, y_peer(y)))
     give_values(28, 40)
     input_grad(2, 4)
 
@@ -330,31 +340,31 @@
 
     lax.fori_loop(1, RING, add2, 0)
     r3[cz] = s3[...]
-    ring(RING, cz, lambda z: send(s3, r3.at[cz], 11, z_peer(z)))
+    ring(cz, lambda z: send(s3, r3.at[cz], 11, z_peer(z)))
     drain(a2r.at[pl.ds(0, RING - 1)], rs.at[10])
     a3s[...] = ((a2r[0] + a2r[1]) + (a2r[2] + a2r[3])) + ((a2r[4] + a2r[5]) + (a2r[6] + a2r[7]))
-    a3r[cz] = a3s[...]
-    ring(RING, cz, lambda z: send(a3s, a3r.at[cz], 12, z_peer(z)))
+    a3r[cx] = a3s[...]
+    ring(cx, lambda x: send(a3s, a3r.at[cx], 12, x_peer(x)))
     give_values(40, 52)
     input_grad(4, 6)
 
     drain(r3.at[pl.ds(0, RING - 1)], rs.at[11])
     total = ((r3[0] + r3[1]) + (r3[2] + r3[3])) + ((r3[4] + r3[5]) + (r3[6] + r3[7]))
     q2[se] = (total * scale).astype(BF16)
-    ring(RING, se, lambda s: send(q2.at[se], q2.at[se], 13, second_peer(s)))
+    ring(se, lambda s: send(q2.at[se], q2.at[se], 13, second_peer(s)))
     drain(a3r.at[pl.ds(0, RING - 1)], rs.at[12])
     aux = ((a3r[0] + a3r[1]) + (a3r[2] + a3r[3])) + ((a3r[4] + a3r[5]) + (a3r[6] + a3r[7]))
     aux = aux * scale
     d4s[...] = aux[0]
-    d4r[cx] = aux[0]
-    ring(RING, cx, lambda x: send(d4s, d4r.at[cx], 14, x_peer(x)))
+    d4r[cz] = aux[0]
+    ring(cz, lambda z: send(d4s, d4r.at[cz], 14, z_peer(z)))
     give_values(52, NT)
     input_grad(6, 8)
     small = aux[1]
 
     drain(q2.at[pl.ds(0, RING - 1)], rs.at[13])
     send(q2, p0.at[fi], 15, partner, fr.at[fi])
-    ring(RING, fi, lambda f: send(q2, q1.at[fi], 16, first_peer(f), fs.at[fi]))
+    ring(fi, lambda f: send(q2, q1.at[fi], 16, first_peer(f), fs.at[fi]))
     q1[fi] = q2[...]
 
     hi = small.astype(BF16)
@@ -377,18 +387,26 @@
     for k in range(8):
         wg[256:264, 128 * k : 128 * (k + 1)] = d4r[k]
 
+    mine = pl.multiple_of(core * 128, 128)
+    other = pl.multiple_of((1 - core) * 128, 128)
+
+    def keep_piece(first, f, piece):
+        wg[pl.ds(first, 128), pl.ds(pl.multiple_of(f * 128, 128), 128)] = piece[f].reshape(128, 128).astype(F32)
+
     def pass_on(f):
         drain(q1.at[f], fs.at[f])
         send(q1.at[f], p0.at[f], 15, partner, fr.at[f])
-
-    ring(RING, fi, pass_on)
-    mine = pl.multiple_of(core * 128, 128)
-    other = pl.multiple_of((1 - core) * 128, 128)
-    for k in range(8):
-        wg[pl.ds(mine, 128), 128 * k : 128 * (k + 1)] = q1[k].reshape(128, 128).astype(F32)
-    for k in range(8):
-        drain(p0.at[k], fr.at[k])
-        wg[pl.ds(other, 128), 128 * k : 128 * (k + 1)] = p0[k].reshape(128, 128).astype(F32)
+        keep_piece(mine, f, q1)
+
+    def take(f):
+        drain(p0.at[f], fr.at[f])
+        keep_piece(other, f, p0)
+
+    keep_piece(mine, fi, q1)
+    near_ring(fi, pass_on)
+    partner_fi = (1 - core) * cy + core * cx
+    take(partner_fi)
+    near_ring(partner_fi, take)
 
     own_v.wait()
     drain(vs.at[:, pl.ds(0, NT - 1)], rs.at[4])

time: 107 us -> 103 us (0.963)
  Pallas kernels: 106 us -> 102 us
    pallas_call x1, Pallas kernels: 105 us -> 100 us  [on_device(): pl.pallas_call(kernel, name='mixer_backward', out_shape=(v((pixels, 8, da...]
where the time goes in v3:
time: 103 us; the launch traced here: 102 us
  Pallas kernels  102 us (99%)
    pallas_call x1, Pallas kernels, on_device(): pl.pallas_call(kernel, name='mixer_backward', out_shape=(v((pixels, 8, da...  100 us

profile of v3, /device:TPU:1, one launch (start us, length us, event | category | flops | bytes accessed | tf_op | source)
XLA Modules:
  0.0 102.5 jit_solution(4621209621292339860)
XLA Ops:
  0.6 100.4 %mixer_backward.1 = (bf16[64,8,4,128]{3,2,1,0:T(4,128)(2,1)S(1)}, bf16[8,64,4,128]{3,2,1,0:T(4,128)(2,1)S(1)}, f32[264,1024]{1,0:T(8,128)S(1)}, f32[2,1024]{1,0:T(2,128)S(1)}, f32[3,8]{1,0:T(4,128)S(1)}) custom-call(bf16[64,8,4,128]{3,2,1,0:T(4,128)(2,1)} %bitcast.19, bf16[64,8,4,128]{3,2,1,0:T(4,128)(2,1)} %bitcast.20, bf16[64,8,4,128]{3,2,1,0:T(4,128)(2,1)} %bitcast.21, ...), custom_call_target="tpu_custom_call" | custom-call | tf_op jit(solution)/shard_map/mixer_backward/pallas_call | solution.py:478
  101.0 1.5 %write_outputs.1 = (bf16[64,8,4,128]{3,2,1,0:T(4,128)(2,1)}, bf16[64,8,4,128]{3,2,1,0:T(4,128)(2,1)}, f32[264,1024]{1,0:T(8,128)}, f32[2,1024]{1,0:T(2,128)}, f32[3,8]{1,0:T(4,128)}) custom-call(bf16[64,8,4,128]{3,2,1,0:T(4,128)(2,1)S(1)} %get-tuple-element.15.vi, bf16[8,64,4,128]{3,2,1,0:T(4,128)(2,1)S(1)} %get-tuple-element.16.ii, ...), custom_call_target="tpu_custom_call" | custom-call | tf_op jit(solution)/shard_map/write_outputs/pallas_call | solution.py:495

commit v4 on v3

--- a/solution.py
+++ b/solution.py
@@ -12,7 +12,7 @@
 NEG_FILL = -1e30
 NT = 64
 RING = 8
-EARLY = 6
+EARLY = 7
 OWN = 46
 LEN = 256
 

time: 103 us -> 104 us (level)
    pallas_call x1, Pallas kernels: 100 us -> 102 us  [on_device(): pl.pallas_call(kernel, name='mixer_backward', out_shape=(v((pixels, 8, da...]
where the time goes in v4:
time: 104 us
  Pallas kernels  103 us (99%)
    pallas_call x1, Pallas kernels, on_device(): pl.pallas_call(kernel, name='mixer_backward', out_shape=(v((pixels, 8, da...  102 us

profile of v4, /device:TPU:1, one launch (start us, length us, event | category | flops | bytes accessed | tf_op | source)
XLA Modules:
  0.0 104.1 jit_solution(10231966266254145315)
XLA Ops:
  0.6 101.9 %mixer_backward.1 = (bf16[64,8,4,128]{3,2,1,0:T(4,128)(2,1)S(1)}, bf16[8,64,4,128]{3,2,1,0:T(4,128)(2,1)S(1)}, f32[264,1024]{1,0:T(8,128)S(1)}, f32[2,1024]{1,0:T(2,128)S(1)}, f32[3,8]{1,0:T(4,128)S(1)}) custom-call(bf16[64,8,4,128]{3,2,1,0:T(4,128)(2,1)} %bitcast.19, bf16[64,8,4,128]{3,2,1,0:T(4,128)(2,1)} %bitcast.20, bf16[64,8,4,128]{3,2,1,0:T(4,128)(2,1)} %bitcast.21, ...), custom_call_target="tpu_custom_call" | custom-call | tf_op jit(solution)/shard_map/mixer_backward/pallas_call | solution.py:478
  102.6 1.5 %write_outputs.1 = (bf16[64,8,4,128]{3,2,1,0:T(4,128)(2,1)}, bf16[64,8,4,128]{3,2,1,0:T(4,128)(2,1)}, f32[264,1024]{1,0:T(8,128)}, f32[2,1024]{1,0:T(2,128)}, f32[3,8]{1,0:T(4,128)}) custom-call(bf16[64,8,4,128]{3,2,1,0:T(4,128)(2,1)S(1)} %get-tuple-element.15.vi, bf16[8,64,4,128]{3,2,1,0:T(4,128)(2,1)S(1)} %get-tuple-element.16.ii, ...), custom_call_target="tpu_custom_call" | custom-call | tf_op jit(solution)/shard_map/write_outputs/pallas_call | solution.py:495
